TPU v7x, 32 devices: a whole 2x2x4 slice. The times are simulated.
32 devices in a mesh: img: 2 (over y), row: 4 (over x, core), col: 4 (over z).
Axes of the slice: x: 2, y: 2, z: 4, core: 2. Of those that a mesh axis runs over, the one named last changes fastest.
Arguments:
- tokens: bfloat16 [4112, 1024], P(('img', 'row'), 'col'), may hold values from -6 to 6
- attn_bias: bfloat16 [16, 257, 257], P('col'), may hold values from -5 to 250
- first_gain: float32 [1024], P('col'), may hold values from 0.5 to 1.5
- first_shift: float32 [1024], P('col'), may hold values from -3 to 3
- qkv_weight: bfloat16 [1024, 3, 1024], P('row', None, 'col'), may hold values from -0.1875 to 0.1875
- qkv_bias: float32 [2, 1024], P(None, 'col'), may hold values from -3 to 3
- proj_weight: bfloat16 [1024, 1024], P('row', 'col'), may hold values from -0.75 to 0.75
- proj_bias: float32 [1024], P('col'), may hold values from -3 to 3
- scale_attn: float32 [1024], P('col'), may hold values from 0.5 to 2
- second_gain: float32 [1024], P('col'), may hold values from 0.5 to 1.5
- second_shift: float32 [1024], P('col'), may hold values from -3 to 3
- fc1_weight: bfloat16 [1024, 4096], P('row', 'col'), may hold values from -0.1875 to 0.1875
- fc1_bias: float32 [4096], P('col'), may hold values from -3 to 3
- fc2_weight: bfloat16 [1024, 4096], P('row', 'col'), may hold values from -0.09375 to 0.09375
- fc2_bias: float32 [1024], P('col'), may hold values from -3 to 3
- scale_mlp: float32 [1024], P('col'), may hold values from 0.5 to 2
- cotangent: float32 [4112, 1024], P(('img', 'row'), 'col'), may hold values from -6 to 6
Outputs:
- out_y: float32 [4112, 1024], P(('img', 'row'), 'col')
- grad_tokens: float32 [4112, 1024], P(('img', 'row'), 'col')
- grad_qkv_weight: float32 [1024, 3, 1024], P('row', None, 'col')
- grad_qkv_bias: float32 [2, 1024], P(None, 'col')
- grad_proj_weight: float32 [1024, 1024], P('row', 'col')
- grad_proj_bias: float32 [1024], P('col')
- grad_scale_attn: float32 [1024], P('col')
- grad_fc1_weight: float32 [1024, 4096], P('row', 'col')
- grad_fc1_bias: float32 [4096], P('col')
- grad_fc2_weight: float32 [1024, 4096], P('row', 'col')
- grad_fc2_bias: float32 [1024], P('col')
- grad_scale_mlp: float32 [1024], P('col')
- grad_first_gain: float32 [1024], P('col')
- grad_first_shift: float32 [1024], P('col')
- grad_second_gain: float32 [1024], P('col')
- grad_second_shift: float32 [1024], P('col')
All inputs are finite; a program needn't handle non-finite values.
Results may differ from a plain program's by a relative error of at most 0.019.
Values may be sent and summed in bfloat16 or wider, within the bound.
No kernel may reach another device: no remote copies, remote signals or barrier semaphores. Data moves between devices by JAX's collectives and lax.ppermute only.
A program may use at most 128 MiB of HBM per device.

v0:
```python
import jax
import jax.numpy as jnp
from jax import lax
from jax.sharding import PartitionSpec as P

HEAD_DIM = 64
D = 1024
SEQ = 257
EPS = 1e-06
SQRT_HALF = 0.7071067811865476
INV_ROOT_TWO_PI = 0.3989422804014327


def gather_cols(values):
    return lax.all_gather(values, "col", axis=1, tiled=True)


def sum_cols(term):
    return lax.psum_scatter(
        term.astype(jnp.bfloat16), "col", scatter_dimension=1, tiled=True
    ).astype(jnp.float32)


def row_totals(sum_one, sum_two):
    return lax.psum((sum_one, sum_two), "col")


def norm_shard(values, gain, shift):
    totals = row_totals(
        jnp.sum(values, axis=1, keepdims=True), jnp.sum(values * values, axis=1, keepdims=True)
    )
    row_mean = totals[0] / D
    row_var = totals[1] / D - row_mean * row_mean
    inv_std = lax.rsqrt(row_var + EPS)
    x_hat = (values - row_mean) * inv_std
    return (x_hat, inv_std, (x_hat * gain + shift).astype(jnp.bfloat16))


def norm_back(grad_in, x_hat, inv_std, gain):
    scaled = grad_in * gain
    totals = row_totals(
        jnp.sum(scaled, axis=1, keepdims=True), jnp.sum(scaled * x_hat, axis=1, keepdims=True)
    )
    return inv_std * (scaled - totals[0] / D - x_hat * (totals[1] / D))


def contract_last(left, right):
    return lax.dot_general(
        left, right, (((1,), (1,)), ((), ())), preferred_element_type=jnp.float32
    )


def contract_first(left, right):
    return lax.dot_general(
        left, right, (((0,), (0,)), ((), ())), preferred_element_type=jnp.float32
    )


def gelu_value(pre_act):
    return 0.5 * pre_act * (1.0 + lax.erf(pre_act * SQRT_HALF))


def gelu_slope(pre_act):
    return (
        0.5 * (1.0 + lax.erf(pre_act * SQRT_HALF))
        + pre_act * jnp.exp(-0.5 * pre_act * pre_act) * INV_ROOT_TWO_PI
    )


def split_heads(heads_in, images, head_count):
    head_grid = heads_in.reshape(images, SEQ, 3, head_count, HEAD_DIM)
    return (head_grid[:, :, 0], head_grid[:, :, 1], head_grid[:, :, 2])


def score_block(query_heads, key_heads, bias_f, score_scale):
    return (
        jnp.einsum("gqhe,gkhe->ghqk", query_heads, key_heads, preferred_element_type=jnp.float32)
        * score_scale
        + bias_f
    )


def attend(heads_in, bias_f, images, head_count, score_scale):
    query_heads, key_heads, value_heads = split_heads(heads_in, images, head_count)
    scores = score_block(query_heads, key_heads, bias_f, score_scale)
    row_max = jnp.max(scores, axis=-1, keepdims=True)
    log_total = row_max + jnp.log(jnp.sum(jnp.exp(scores - row_max), axis=-1, keepdims=True))
    weights_half = jnp.exp(scores - log_total).astype(jnp.bfloat16)
    output = jnp.einsum(
        "ghqk,gkhe->gqhe", weights_half, value_heads, preferred_element_type=jnp.float32
    )
    return (output.reshape(images * SEQ, head_count * HEAD_DIM).astype(jnp.bfloat16), log_total)


def attend_back(heads_in, bias_f, log_total, grad_heads, images, head_count, score_scale):
    query_heads, key_heads, value_heads = split_heads(heads_in, images, head_count)
    scores = score_block(query_heads, key_heads, bias_f, score_scale)
    prob_full = jnp.exp(scores - log_total)
    prob_half = prob_full.astype(jnp.bfloat16)
    grad_out = grad_heads.reshape(images, SEQ, head_count, HEAD_DIM)
    grad_value = jnp.einsum(
        "ghqk,gqhe->gkhe", prob_half, grad_out, preferred_element_type=jnp.float32
    )
    grad_prob = jnp.einsum(
        "gqhe,gkhe->ghqk", grad_out, value_heads, preferred_element_type=jnp.float32
    )
    row_dot = jnp.sum(prob_full * grad_prob, axis=-1, keepdims=True)
    grad_s = (prob_full * (grad_prob - row_dot)).astype(jnp.bfloat16)
    grad_query = (
        jnp.einsum("ghqk,gkhe->gqhe", grad_s, key_heads, preferred_element_type=jnp.float32)
        * score_scale
    )
    grad_key = (
        jnp.einsum("ghqk,gqhe->gkhe", grad_s, query_heads, preferred_element_type=jnp.float32)
        * score_scale
    )
    flat_shape = (images * SEQ, head_count * HEAD_DIM)
    stacked = jnp.stack(
        [
            grad_query.reshape(flat_shape),
            grad_key.reshape(flat_shape),
            grad_value.reshape(flat_shape),
        ],
        axis=1,
    )
    return stacked.astype(jnp.bfloat16)


def body(
    tokens,
    attn_bias,
    first_gain,
    first_shift,
    qkv_weight,
    qkv_bias,
    proj_weight,
    proj_bias,
    scale_attn,
    second_gain,
    second_shift,
    fc1_weight,
    fc1_bias,
    fc2_weight,
    fc2_bias,
    scale_mlp,
    cotangent,
):
    count_rows = tokens.shape[0]
    images = count_rows // SEQ
    head_count = qkv_weight.shape[2] // HEAD_DIM
    score_scale = HEAD_DIM ** (-0.5)
    bias_f = attn_bias.astype(jnp.float32)[None]
    qkv_full, proj_full, hidden_full, output_full = (
        lax.all_gather(qkv_weight, "row", axis=0, tiled=True),
        lax.all_gather(proj_weight, "row", axis=0, tiled=True),
        lax.all_gather(fc1_weight, "row", axis=0, tiled=True),
        lax.all_gather(fc2_weight, "row", axis=0, tiled=True),
    )
    x_val = tokens.astype(jnp.float32)
    hat_first, inv_first, first_local = norm_shard(x_val, first_gain, first_shift)
    first_norm = gather_cols(first_local)
    mixed_all = jnp.einsum("rd,djo->rjo", first_norm, qkv_full, preferred_element_type=jnp.float32)
    heads_in = jnp.stack(
        [mixed_all[:, 0] + qkv_bias[0], mixed_all[:, 1], mixed_all[:, 2] + qkv_bias[1]], axis=1
    ).astype(jnp.bfloat16)
    attn_out, log_total = attend(heads_in, bias_f, images, head_count, score_scale)
    proj_val = sum_cols(contract_last(attn_out, proj_full)) + proj_bias
    x_mid = x_val + scale_attn * proj_val
    hat_second, inv_second, second_local = norm_shard(x_mid, second_gain, second_shift)
    second_norm = gather_cols(second_local)
    pre_act = jnp.dot(second_norm, hidden_full, preferred_element_type=jnp.float32) + fc1_bias
    act_val = gelu_value(pre_act).astype(jnp.bfloat16)
    mlp_val = sum_cols(contract_last(act_val, output_full)) + fc2_bias
    out_y = x_mid + scale_mlp * mlp_val
    qkv_back, proj_back, hidden_back, output_back = (
        lax.all_gather(qkv_weight, "row", axis=0, tiled=True),
        lax.all_gather(proj_weight, "row", axis=0, tiled=True),
        lax.all_gather(fc1_weight, "row", axis=0, tiled=True),
        lax.all_gather(fc2_weight, "row", axis=0, tiled=True),
    )
    grad_mlp = gather_cols((cotangent * scale_mlp).astype(jnp.bfloat16))
    grad_act = jnp.dot(grad_mlp, output_back, preferred_element_type=jnp.float32)
    grad_pre = (grad_act * gelu_slope(pre_act)).astype(jnp.bfloat16)
    grad_two = sum_cols(contract_last(grad_pre, hidden_back))
    grad_mid = cotangent + norm_back(grad_two, hat_second, inv_second, second_gain)
    grad_attn_in = gather_cols((grad_mid * scale_attn).astype(jnp.bfloat16))
    grad_heads = jnp.dot(grad_attn_in, proj_back, preferred_element_type=jnp.float32).astype(
        jnp.bfloat16
    )
    grad_qkv = attend_back(heads_in, bias_f, log_total, grad_heads, images, head_count, score_scale)
    grad_one = sum_cols(
        jnp.einsum("rjo,djo->rd", grad_qkv, qkv_back, preferred_element_type=jnp.float32)
    )
    grad_tokens = grad_mid + norm_back(grad_one, hat_first, inv_first, first_gain)
    grad_terms = (
        jnp.einsum("rd,rjo->djo", first_norm, grad_qkv, preferred_element_type=jnp.float32),
        contract_first(grad_attn_in, attn_out),
        contract_first(second_norm, grad_pre),
        contract_first(grad_mlp, act_val),
    )
    shares = (
        lax.psum_scatter(
            grad_terms[0].astype(jnp.bfloat16), "row", scatter_dimension=0, tiled=True
        ).astype(jnp.float32),
        lax.psum_scatter(
            grad_terms[1].astype(jnp.bfloat16), "row", scatter_dimension=0, tiled=True
        ).astype(jnp.float32),
        lax.psum_scatter(
            grad_terms[2].astype(jnp.bfloat16), "row", scatter_dimension=0, tiled=True
        ).astype(jnp.float32),
        lax.psum_scatter(
            grad_terms[3].astype(jnp.bfloat16), "row", scatter_dimension=0, tiled=True
        ).astype(jnp.float32),
    )
    weight_grads = (
        lax.psum(shares[0].astype(jnp.bfloat16), "img").astype(jnp.float32),
        lax.psum(shares[1].astype(jnp.bfloat16), "img").astype(jnp.float32),
        lax.psum(shares[2].astype(jnp.bfloat16), "img").astype(jnp.float32),
        lax.psum(shares[3].astype(jnp.bfloat16), "img").astype(jnp.float32),
    )
    grad_qkv_f = grad_qkv.astype(jnp.float32)
    small_sums = lax.psum(
        (
            jnp.stack(
                [jnp.sum(grad_qkv_f[:, 0], axis=0), jnp.sum(grad_qkv_f[:, 2], axis=0)], axis=0
            ),
            jnp.sum(grad_mid * scale_attn, axis=0),
            jnp.sum(grad_mid * proj_val, axis=0),
            jnp.sum(grad_pre.astype(jnp.float32), axis=0),
            jnp.sum(cotangent * scale_mlp, axis=0),
            jnp.sum(cotangent * mlp_val, axis=0),
            jnp.sum(grad_one * hat_first, axis=0),
            jnp.sum(grad_one, axis=0),
            jnp.sum(grad_two * hat_second, axis=0),
            jnp.sum(grad_two, axis=0),
        ),
        ("img", "row"),
    )
    return (
        out_y,
        grad_tokens,
        weight_grads[0],
        small_sums[0],
        weight_grads[1],
        small_sums[1],
        small_sums[2],
        weight_grads[2],
        small_sums[3],
        weight_grads[3],
        small_sums[4],
        small_sums[5],
        small_sums[6],
        small_sums[7],
        small_sums[8],
        small_sums[9],
    )


def solution(mesh):
    return jax.shard_map(
        body,
        mesh=mesh,
        in_specs=(
            P(("img", "row"), "col"),
            P("col", None, None),
            P("col"),
            P("col"),
            P("row", None, "col"),
            P(None, "col"),
            P("row", "col"),
            P("col"),
            P("col"),
            P("col"),
            P("col"),
            P("row", "col"),
            P("col"),
            P("row", "col"),
            P("col"),
            P("col"),
            P(("img", "row"), "col"),
        ),
        out_specs=(
            P(("img", "row"), "col"),
            P(("img", "row"), "col"),
            P("row", None, "col"),
            P(None, "col"),
            P("row", "col"),
            P("col"),
            P("col"),
            P("row", "col"),
            P("col"),
            P("row", "col"),
            P("col"),
            P("col"),
            P("col"),
            P("col"),
            P("col"),
            P("col"),
        ),
        check_vma=False,
    )
```

profile of v0, /device:TPU:0, one launch (start us, length us, event | category | flops | bytes accessed | tf_op | source)
XLA Modules:
  0.0 541.6 jit_solution(1392354417559982249)
XLA Ops:
  7.2 1.2 convert_reduce_fusion.1
  8.5 13.7 %all-reduce.4 = (f32[514,1]{0,1:T(1,128)S(1)}, f32[514,1]{0,1:T(1,128)S(1)}) all-reduce(f32[514,1]{0,1:T(1,128)S(1)} %broadcast_in_dim.16, f32[514,1]{0,1:T(1,128)S(1)} %broadcast_in_dim.17), channel_id=1, replica_groups=mesh['img'=2,'row'=4,'col'=4] {'col'}, use_global_device_ids=true, to_apply=%region_1.0 | all-reduce | flops 1028 | bytes 8224 | tf_op jit(solution)/shard_map/psum | solution.py:25
  22.3 1.9 fusion.37
  25.0 3.1 copy.51
  28.1 7.6 %all_gather.30 = bf16[1024,256]{1,0:T(8,128)(2,1)} all-gather(bf16[256,256]{1,0:T(8,128)(2,1)S(1)} %copy-done.15), channel_id=1, replica_groups=mesh['img'=2,'row'=4,'col'=4] {'row'}, dimensions={0}, use_global_device_ids=true | all-gather | bytes 655360 | tf_op jit(solution)/shard_map/all_gather | solution.py:155
  35.7 17.0 %all-gather.8.cloned.1.call-done = bf16[514,1024]{1,0:T(8,128)(2,1)} async-done(((bf16[514,256]{1,0:T(8,128)(2,1)}), bf16[514,1024]{1,0:T(8,128)(2,1)}) %all-gather.8.cloned.1.call-update) | async-done | bytes 1052688 | tf_op jit(solution)/shard_map/all_gather | solution.py:15
  52.7 19.5 %all-gather.10.cloned.1.call-done = bf16[1024,3,256]{2,0,1:T(8,128)(2,1)} async-done(((bf16[256,3,256]{2,0,1:T(8,128)(2,1)}), bf16[1024,3,256]{2,0,1:T(8,128)(2,1)}) %all-gather.10.cloned.1.call-update) | async-done | bytes 1572880 | tf_op jit(solution)/shard_map/all_gather | solution.py:154
  72.2 2.7 fusion.15
  75.4 1.1 copy.49
  76.7 1.1 copy.50
  78.1 1.1 copy.52
  79.2 2.6 fusion
  84.7 1.1 copy.54
  85.9 2.1 convert_element_type.114
  87.9 2.7 convolution_convert_fusion.5
  91.3 27.3 %reduce-scatter.9.cloned.1.call-done = bf16[514,256]{1,0:T(8,128)(2,1)} async-done(((bf16[514,1024]{1,0:T(8,128)(2,1)}), bf16[514,256]{1,0:T(8,128)(2,1)}) %reduce-scatter.9.cloned.1.call-update) | async-done | bytes 263184 | tf_op jit(solution)/shard_map/reduce_scatter | solution.py:19
  118.6 1.2 fusion.41
  119.8 10.0 %all-reduce.3 = (f32[514,1]{0,1:T(1,128)}, f32[514,1]{0,1:T(1,128)}) all-reduce(f32[514,1]{0,1:T(1,128)S(1)} %broadcast_in_dim.18, f32[514,1]{0,1:T(1,128)S(1)} %broadcast_in_dim.19), channel_id=1, replica_groups=mesh['img'=2,'row'=4,'col'=4] {'col'}, use_global_device_ids=true, to_apply=%region_8.0 | all-reduce | flops 1028 | bytes 8224 | tf_op jit(solution)/shard_map/psum | solution.py:25
  130.5 1.9 add_convert_fusion
  132.5 1.8 multiply_convert_fusion.3
  135.3 5.8 %all-gather.14.cloned.1.call-done = bf16[1024,1024]{1,0:T(8,128)(2,1)} async-done(((bf16[256,1024]{1,0:T(8,128)(2,1)}), bf16[1024,1024]{1,0:T(8,128)(2,1)}) %all-gather.14.cloned.1.call-update) | async-done | bytes 2097168 | tf_op jit(solution)/shard_map/all_gather | solution.py:156
  141.1 32.2 %all-gather.12.cloned.1.call-done = bf16[514,1024]{1,0:T(8,128)(2,1)} async-done(((bf16[514,256]{1,0:T(8,128)(2,1)}), bf16[514,1024]{1,0:T(8,128)(2,1)}) %all-gather.12.cloned.1.call-update) | async-done | bytes 1052688 | tf_op jit(solution)/shard_map/all_gather | solution.py:15
  173.3 4.9 multiply_convert_fusion.1
  178.2 25.6 %all-gather.18.cloned.1.call-done = bf16[514,1024]{1,0:T(8,128)(2,1)} async-done(((bf16[514,256]{1,0:T(8,128)(2,1)}), bf16[514,1024]{1,0:T(8,128)(2,1)}) %all-gather.18.cloned.1.call-update) | async-done | bytes 1052688 | tf_op jit(solution)/shard_map/all_gather | solution.py:15
  203.8 22.5 %all-gather.16.cloned.1.call-done = bf16[1024,1024]{1,0:T(8,128)(2,1)} async-done(((bf16[256,1024]{1,0:T(8,128)(2,1)}), bf16[1024,1024]{1,0:T(8,128)(2,1)}) %all-gather.16.cloned.1.call-update) | async-done | bytes 2097168 | tf_op jit(solution)/shard_map/all_gather | solution.py:157
  226.2 5.2 convert_reduce_fusion
  231.4 1.0 copy-done.31
  232.4 2.3 convolution_convert_fusion.3
  234.8 4.2 convolution_convert_fusion.4
  239.1 23.5 %reduce-scatter.13.cloned.1.call-done = bf16[514,256]{1,0:T(8,128)(2,1)} async-done(((bf16[514,1024]{1,0:T(8,128)(2,1)}), bf16[514,256]{1,0:T(8,128)(2,1)}) %reduce-scatter.13.cloned.1.call-update) | async-done | bytes 263184 | tf_op jit(solution)/shard_map/reduce_scatter | solution.py:19
  262.6 2.1 fusion.31
  264.7 10.0 %all-reduce.2 = (f32[514,1]{0,1:T(1,128)}, f32[514,1]{0,1:T(1,128)}) all-reduce(f32[514,1]{0,1:T(1,128)S(1)} %broadcast_in_dim.21, f32[514,1]{0,1:T(1,128)S(1)} %broadcast_in_dim.20), channel_id=1, replica_groups=mesh['img'=2,'row'=4,'col'=4] {'col'}, use_global_device_ids=true, to_apply=%region_16.0 | all-reduce | flops 1028 | bytes 8224 | tf_op jit(solution)/shard_map/psum | solution.py:25
  275.4 15.9 %reduce-scatter.11.cloned.1.call-done = bf16[514,256]{1,0:T(8,128)(2,1)} async-done(((bf16[514,1024]{1,0:T(8,128)(2,1)}), bf16[514,256]{1,0:T(8,128)(2,1)}) %reduce-scatter.11.cloned.1.call-update) | async-done | bytes 263184 | tf_op jit(solution)/shard_map/reduce_scatter | solution.py:19
  291.3 3.1 multiply_reduce_fusion.2
  296.0 4.7 convolution_convert_fusion
  300.8 4.8 convolution_convert_fusion.1
  306.0 18.9 %all-gather.20.cloned.1.call-done = bf16[514,1024]{1,0:T(8,128)(2,1)} async-done(((bf16[514,256]{1,0:T(8,128)(2,1)}), bf16[514,1024]{1,0:T(8,128)(2,1)}) %all-gather.20.cloned.1.call-update) | async-done | bytes 1052688 | tf_op jit(solution)/shard_map/all_gather | solution.py:15
  324.8 2.5 convolution_convert_fusion.9
  327.3 2.1 reshape.89
  329.4 2.1 copy.56
  331.5 2.8 convolution_convert_fusion.6
  334.2 3.2 fusion.11
  337.5 2.8 multiply_reduce_fusion
  340.3 3.7 multiply_convert_fusion
  344.0 1.2 copy-done.4
  345.2 1.3 fusion.13
  347.2 1.4 copy.74
  348.6 1.1 reshape.83
  351.2 1.0 constant_dynamic-update-slice_fusion.2
  352.3 4.0 convolution_convert_fusion.2
  356.3 2.0 bitcast_convert_fusion
  358.4 32.0 %reduce-scatter.21.cloned.1.call-done = bf16[256,1024]{1,0:T(8,128)(2,1)} async-done(((bf16[1024,1024]{1,0:T(8,128)(2,1)}), bf16[256,1024]{1,0:T(8,128)(2,1)}) %reduce-scatter.21.cloned.1.call-update) | async-done | bytes 524304 | tf_op jit(solution)/shard_map/reduce_scatter | solution.py:208
  390.5 24.7 %reduce-scatter.19.cloned.1.call-done = bf16[256,256]{1,0:T(8,128)(2,1)} async-done(((bf16[1024,256]{1,0:T(8,128)(2,1)}), bf16[256,256]{1,0:T(8,128)(2,1)}) %reduce-scatter.19.cloned.1.call-update) | async-done | bytes 131088 | tf_op jit(solution)/shard_map/reduce_scatter | solution.py:205
  415.2 30.4 %reduce-scatter.17.cloned.1.call-done = bf16[256,3,256]{2,0,1:T(8,128)(2,1)} async-done(((bf16[1024,3,256]{2,0,1:T(8,128)(2,1)}), bf16[256,3,256]{2,0,1:T(8,128)(2,1)}) %reduce-scatter.17.cloned.1.call-update) | async-done | bytes 393232 | tf_op jit(solution)/shard_map/reduce_scatter | solution.py:202
  446.0 29.5 %reduce-scatter.15.cloned.1.call-done = bf16[514,256]{1,0:T(8,128)(2,1)} async-done(((bf16[514,1024]{1,0:T(8,128)(2,1)}), bf16[514,256]{1,0:T(8,128)(2,1)}) %reduce-scatter.15.cloned.1.call-update) | async-done | bytes 263184 | tf_op jit(solution)/shard_map/reduce_scatter | solution.py:19
  475.6 1.4 fusion.32
  477.1 24.8 %all-reduce = (f32[2,256]{1,0:T(2,128)}, f32[256]{0:T(256)}, f32[256]{0:T(256)}, f32[1024]{0:T(1024)}, f32[256]{0:T(256)}, /*index=5*/f32[256]{0:T(256)}, f32[25...) all-reduce(f32[2,256]{1,0:T(2,128)S(1)} %pad_maximum_fusion, ...), channel_id=1, replica_groups=mesh['img'=2,'row'=4,'col'=4] {'img','row'}, use_global_device_ids=true, to_apply=%region_27.0 | all-reduce | flops 3584 | bytes 28672 | tf_op jit(solution)/shard_map/psum | solution.py:222
  501.8 9.1 %all-reduce.1 = (f32[514,1]{0,1:T(1,128)S(1)}, f32[514,1]{0,1:T(1,128)S(1)}) all-reduce(f32[514,1]{0,1:T(1,128)S(1)} %broadcast_in_dim.23, f32[514,1]{0,1:T(1,128)S(1)} %broadcast_in_dim.22), channel_id=1, replica_groups=mesh['img'=2,'row'=4,'col'=4] {'col'}, use_global_device_ids=true, to_apply=%region_22.0 | all-reduce | flops 1028 | bytes 8224 | tf_op jit(solution)/shard_map/psum | solution.py:25
  511.0 2.1 fusion.25
  513.1 15.1 %all-reduce.8.cloned.1.call-done = (bf16[256,3,256]{2,0,1:T(8,128)(2,1)}, bf16[256,256]{1,0:T(8,128)(2,1)}, bf16[256,1024]{1,0:T(8,128)(2,1)}, bf16[256,1024]{1,0:T(8,128)(2,1)}) async-done(((bf16[256,3,256]{2,0,1:T(8,128)(2,1)}, bf16[256,256]{1,0:T(8,128)(2,1)}, bf16[256,1024]{1,0:T(8,128)(2,1)}, bf16[256,1024]{1,0:T(8,128)(2,1)}), (bf16[256,3,256]{2,0,1:T(8,128)(2,1)}, bf16[256,256]{1,0:T(8,128)(2,1)}, ...) | async-done | bytes 1572880 | tf_op jit(solution)/shard_map/psum | solution.py:216
  528.2 1.7 convert_element_type.134
  529.9 1.9 convert_element_type.131
  531.8 2.1 convert_element_type.136
  533.9 1.1 convert_element_type.139
  (129 shorter events, 12.7 us)
Async XLA Ops:
  7.2 20.9 %copy-start.15 = (bf16[256,256]{1,0:T(8,128)(2,1)S(1)}, bf16[256,256]{1,0:T(8,128)(2,1)}, u32[]{:S(2)}) copy-start(bf16[256,256]{1,0:T(8,128)(2,1)} %param.23) | copy-start | bytes 393220
  7.2 45.5 %all-gather.8.cloned.1.call-start = ((), (), s32[]{:S(2)}) async-start(), calls=%async_computation.8 | async-start | bytes 1331200 | tf_op jit(solution)/shard_map/all_gather | solution.py:15
  22.2 13.5 %copy-start.27 = (f32[2,256]{1,0:T(2,128)S(1)}, f32[2,256]{1,0:T(2,128)}, u32[]{:S(2)}) copy-start(f32[2,256]{1,0:T(2,128)} %param.22) | copy-start | bytes 6148
  24.2 48.1 %all-gather.10.cloned.1.call-start = ((), (), s32[]{:S(2)}) async-start(), calls=%async_computation.9 | async-start | bytes 1966080 | tf_op jit(solution)/shard_map/all_gather | solution.py:154
  24.9 93.6 %reduce-scatter.9.cloned.1.call-start = ((), (), s32[]{:S(2)}) async-start(), calls=%async_computation.10 | async-start | bytes 1331200 | tf_op jit(solution)/shard_map/reduce_scatter | solution.py:19
  79.2 2.6 copy-start
  82.5 1.0 copy-start.8
  83.5 1.2 copy-start.3
  85.9 32.7 %copy-start.2 = (bf16[514,256]{1,0:T(8,128)(2,1)S(1)}, bf16[514,256]{1,0:T(8,128)(2,1)}, u32[]{:S(2)}) copy-start(bf16[514,256]{1,0:T(8,128)(2,1)} %param.17) | copy-start | bytes 789508
  85.9 32.7 %copy-start.16 = (f32[256]{0:T(256)S(1)}, f32[256]{0:T(256)}, u32[]{:S(2)}) copy-start(f32[256]{0:T(256)} %param.25) | copy-start | bytes 3076
  85.9 32.7 %copy-start.17 = (f32[256]{0:T(256)S(1)}, f32[256]{0:T(256)}, u32[]{:S(2)}) copy-start(f32[256]{0:T(256)} %param.24) | copy-start | bytes 3076
  87.9 42.6 %copy-start.18 = (f32[256]{0:T(256)S(1)}, f32[256]{0:T(256)}, u32[]{:S(2)}) copy-start(f32[256]{0:T(256)} %param.26) | copy-start | bytes 3076
  90.7 50.4 %all-gather.14.cloned.1.call-start = ((), (), s32[]{:S(2)}) async-start(), calls=%async_computation.12 | async-start | bytes 2621440 | tf_op jit(solution)/shard_map/all_gather | solution.py:156
  91.2 82.0 %all-gather.12.cloned.1.call-start = ((), (), s32[]{:S(2)}) async-start(), calls=%async_computation.11 | async-start | bytes 1331200 | tf_op jit(solution)/shard_map/all_gather | solution.py:15
  132.4 71.3 %all-gather.18.cloned.1.call-start = ((), (), s32[]{:S(2)}) async-start(), calls=%async_computation.15 | async-start | bytes 1331200 | tf_op jit(solution)/shard_map/all_gather | solution.py:15
  134.3 91.9 %all-gather.16.cloned.1.call-start = ((), (), s32[]{:S(2)}) async-start(), calls=%async_computation.13 | async-start | bytes 2621440 | tf_op jit(solution)/shard_map/all_gather | solution.py:157
  135.1 91.1 %copy-start.30 = (f32[1024]{0:T(1024)S(1)}, f32[1024]{0:T(1024)}, u32[]{:S(2)}) copy-start(f32[1024]{0:T(1024)} %param.29) | copy-start | bytes 12292
  135.1 127.5 %reduce-scatter.13.cloned.1.call-start = ((), (), s32[]{:S(2)}) async-start(), calls=%async_computation.16 | async-start | bytes 1331200 | tf_op jit(solution)/shard_map/reduce_scatter | solution.py:19
  226.2 6.2 %copy-start.28 = (bf16[1024,1024]{1,0:T(8,128)(2,1)S(1)}, bf16[1024,1024]{1,0:T(8,128)(2,1)}, u32[]{:S(2)}) copy-start(bf16[1024,1024]{1,0:T(8,128)(2,1)} %all-gather.14.cloned.1.call-done) | copy-start | bytes 6291460
  231.4 1.0 copy-start.31
  234.7 56.5 %reduce-scatter.11.cloned.1.call-start = ((), (), s32[]{:S(2)}) async-start(), calls=%async_computation.14 | async-start | bytes 1331200 | tf_op jit(solution)/shard_map/reduce_scatter | solution.py:19
  239.1 85.8 %all-gather.20.cloned.1.call-start = ((), (), s32[]{:S(2)}) async-start(), calls=%async_computation.17 | async-start | bytes 1331200 | tf_op jit(solution)/shard_map/all_gather | solution.py:15
  294.4 0.8 copy-start.6
  296.0 62.5 %reduce-scatter.23.cloned.1.call-start = ((), (), s32[]{:S(2)}) async-start(), calls=%async_computation.22 | async-start | bytes 2621440 | tf_op jit(solution)/shard_map/reduce_scatter | solution.py:211
  300.8 89.7 %reduce-scatter.21.cloned.1.call-start = ((), (), s32[]{:S(2)}) async-start(), calls=%async_computation.21 | async-start | bytes 2621440 | tf_op jit(solution)/shard_map/reduce_scatter | solution.py:208
  305.7 109.5 %reduce-scatter.19.cloned.1.call-start = ((), (), s32[]{:S(2)}) async-start(), calls=%async_computation.20 | async-start | bytes 655360 | tf_op jit(solution)/shard_map/reduce_scatter | solution.py:205
  334.2 3.2 copy-start.1
  334.2 3.2 copy-start.9
  334.2 3.2 copy-start.10
  340.3 105.4 %reduce-scatter.17.cloned.1.call-start = ((), (), s32[]{:S(2)}) async-start(), calls=%async_computation.19 | async-start | bytes 1966080 | tf_op jit(solution)/shard_map/reduce_scatter | solution.py:202
  340.3 4.9 copy-start.12
  344.0 1.2 copy-start.4
  345.2 1.3 copy-start.13
  346.5 3.3 copy-start.5
  346.5 3.3 copy-start.11
  352.3 4.0 copy-start.29
  356.3 119.3 %reduce-scatter.15.cloned.1.call-start = ((), (), s32[]{:S(2)}) async-start(), calls=%async_computation.18 | async-start | bytes 1331200 | tf_op jit(solution)/shard_map/reduce_scatter | solution.py:19
  358.4 169.8 %all-reduce.8.cloned.1.call-start = ((), (), s32[]{:S(2)}) async-start(), calls=%async_computation.23 | async-start | bytes 3145728 | tf_op jit(solution)/shard_map/psum | solution.py:216
  445.7 29.9 %copy-start.19 = (f32[256]{0:T(256)S(1)}, f32[256]{0:T(256)}, u32[]{:S(2)}) copy-start(f32[256]{0:T(256)} %param.19) | copy-start | bytes 3076
  445.7 31.3 %copy-start.20 = (f32[256]{0:T(256)S(1)}, f32[256]{0:T(256)}, u32[]{:S(2)}) copy-start(f32[256]{0:T(256)} %get-tuple-element.26) | copy-start | bytes 3076
  445.7 31.3 %copy-start.21 = (f32[256]{0:T(256)S(1)}, f32[256]{0:T(256)}, u32[]{:S(2)}) copy-start(f32[256]{0:T(256)} %get-tuple-element.27) | copy-start | bytes 3076
  445.7 31.3 %copy-start.22 = (f32[256]{0:T(256)S(1)}, f32[256]{0:T(256)}, u32[]{:S(2)}) copy-start(f32[256]{0:T(256)} %get-tuple-element.64) | copy-start | bytes 3076
  445.7 31.3 %copy-start.23 = (f32[256]{0:T(256)S(1)}, f32[256]{0:T(256)}, u32[]{:S(2)}) copy-start(f32[256]{0:T(256)} %get-tuple-element.65) | copy-start | bytes 3076
  445.7 31.3 %copy-start.24 = (f32[256]{0:T(256)S(1)}, f32[256]{0:T(256)}, u32[]{:S(2)}) copy-start(f32[256]{0:T(256)} %get-tuple-element.18) | copy-start | bytes 3076
  445.7 31.3 %copy-start.25 = (f32[256]{0:T(256)S(1)}, f32[256]{0:T(256)}, u32[]{:S(2)}) copy-start(f32[256]{0:T(256)} %get-tuple-element.30) | copy-start | bytes 3076
  445.8 31.3 %copy-start.26 = (f32[1024]{0:T(1024)S(1)}, f32[1024]{0:T(1024)}, u32[]{:S(2)}) copy-start(f32[1024]{0:T(1024)} %get-tuple-element.74) | copy-start | bytes 12292
  445.8 65.2 %copy-start.7 = (f32[514,256]{1,0:T(8,128)S(1)}, f32[514,256]{1,0:T(8,128)}, u32[]{:S(2)}) copy-start(f32[514,256]{1,0:T(8,128)} %copy-done.6) | copy-start | bytes 1579012
  528.2 5.8 %copy-start.14 = (bf16[256,1024]{1,0:T(8,128)(2,1)S(1)}, bf16[256,1024]{1,0:T(8,128)(2,1)}, u32[]{:S(2)}) copy-start(bf16[256,1024]{1,0:T(8,128)(2,1)} %get-tuple-element.59) | copy-start | bytes 1572868
Sparse Core Ops, SparseCore 0:
  24.3 28.3 all-gather.7
  54.3 17.9 all-gather.9
  90.8 27.7 reduce-scatter.8
  120.0 21.0 all-gather.13
  143.0 30.1 all-gather.11
  175.2 28.4 all-gather.17
  205.3 20.8 all-gather.15
  234.9 27.7 reduce-scatter.12
  264.9 26.3 reduce-scatter.10
  296.1 28.7 all-gather.19
  327.4 29.4 reduce-scatter.22
  359.2 31.1 reduce-scatter.20
  393.5 21.6 reduce-scatter.18
  417.6 28.0 reduce-scatter.16
  447.8 27.7 reduce-scatter.14
  477.9 50.2 all-reduce.7
where the time goes:
time: 543 us; the launch traced here: 542 us
  waiting for transfers between devices  342 us (63%)
  blocking collectives  75.2 us (14%)
  matrix products  54 us (10%)
  other arithmetic  31.2 us (6%)
  local copies, waits for them, and re-layouts  23.8 us (4%)
  between operations  14.5 us (3%)
    reduce_scatter x4, waiting for transfers between devices, sum_cols(): lax.psum_scatter(term.astype(jnp.bfloat16), 'col', scatter_dimension=1, t...  96.2 us
    all_gather x4, waiting for transfers between devices, gather_cols(): return lax.all_gather(values, 'col', axis=1, tiled=True)  93.6 us
    psum x4, blocking collectives, row_totals(): return lax.psum((sum_one, sum_two), 'col')  42.8 us
    reduce_scatter x1, waiting for transfers between devices, body(): lax.psum_scatter(grad_terms[2].astype(jnp.bfloat16), 'row', scatter_dimen...  32 us
    reduce_scatter x1, waiting for transfers between devices, body(): lax.psum_scatter(grad_terms[0].astype(jnp.bfloat16), 'row', scatter_dimen...  30.4 us
    psum x1, blocking collectives, body(): lax.psum((jnp.stack([jnp.sum(grad_qkv_f[:, 0], axis=0), jnp.sum(grad_qkv_...  24.8 us
    reduce_scatter x1, waiting for transfers between devices, body(): lax.psum_scatter(grad_terms[1].astype(jnp.bfloat16), 'row', scatter_dimen...  24.7 us
    all_gather x1, waiting for transfers between devices, body(): lax.all_gather(fc2_weight, 'row', axis=0, tiled=True)  22.5 us
  transfers between devices with their start and end apart: 16, of which 15 were waited for; matrix products, arithmetic and copies ran while one was open for 12% of the time, Pallas kernels for 0%

commit v1 on v0

--- a/solution.py
+++ b/solution.py
@@ -11,8 +11,20 @@
 INV_ROOT_TWO_PI = 0.3989422804014327
 
 
+def doubled_up(x, axis, dim):
+    ways, here = (lax.axis_size(axis), lax.axis_index(axis))
+    grown, reach = (x, 1)
+    while reach < ways:
+        theirs = lax.ppermute(grown, axis, [(d, d ^ reach) for d in range(ways)])
+        mine_first = jnp.concatenate([grown, theirs], axis=dim)
+        theirs_first = jnp.concatenate([theirs, grown], axis=dim)
+        grown = jnp.where(here & reach == 0, mine_first, theirs_first)
+        reach = 2 * reach
+    return grown
+
+
 def gather_cols(values):
-    return lax.all_gather(values, "col", axis=1, tiled=True)
+    return doubled_up(values, "col", 1)
 
 
 def sum_cols(term):

time: 543 us -> 484 us (0.89)
  waiting for transfers between devices: 342 us -> 276 us
  starting transfers between devices: 1.05 us -> 8.96 us
    all_gather x4 -> x0, waiting for transfers between devices: 93.6 us -> none  [gather_cols(): return lax.all_gather(values, 'col', axis=1, tiled=True)]
    ppermute x0 -> x8, waiting for transfers between devices: none -> 89.7 us  [doubled_up(): theirs = lax.ppermute(grown, axis, [(d, d ^ reach) for d in range(ways)])]
    reduce_scatter x1, waiting for transfers between devices: 24.7 us -> 0.02 us  [body(): lax.psum_scatter(grad_terms[1].astype(jnp.bfloat16), 'row', scatter_dimen...]
    all_gather x1, waiting for transfers between devices: 22.5 us -> 0.01 us  [body(): lax.all_gather(fc2_weight, 'row', axis=0, tiled=True)]
    all_gather x1, waiting for transfers between devices: 19.5 us -> 0.01 us  [body(): lax.all_gather(qkv_weight, 'row', axis=0, tiled=True)]
    reduce_scatter x1, waiting for transfers between devices: 0.02 us -> 12.3 us  [body(): lax.psum_scatter(grad_terms[3].astype(jnp.bfloat16), 'row', scatter_dimen...]
    ppermute x0 -> x8, starting transfers between devices: none -> 8.25 us  [doubled_up(): theirs = lax.ppermute(grown, axis, [(d, d ^ reach) for d in range(ways)])]
    all_gather x1, waiting for transfers between devices: 5.76 us -> 0.01 us  [body(): lax.all_gather(fc1_weight, 'row', axis=0, tiled=True)]
  transfers between devices with their start and end apart: 16 -> 20, of which waited for: 15 -> 16; matrix products, arithmetic and copies ran while one was open for 12% -> 14% of each run, Pallas kernels for 0% -> 0%
where the time goes in v1:
time: 484 us; the launch traced here: 483 us
  waiting for transfers between devices  276 us (57%)
  blocking collectives  75.6 us (16%)
  matrix products  55 us (11%)
  other arithmetic  27.4 us (6%)
  local copies, waits for them, and re-layouts  25.9 us (5%)
  between operations  14.9 us (3%)
  starting transfers between devices  8.96 us (2%)
    reduce_scatter x4, waiting for transfers between devices, sum_cols(): lax.psum_scatter(term.astype(jnp.bfloat16), 'col', scatter_dimension=1, t...  92.3 us
    ppermute x8, waiting for transfers between devices, doubled_up(): theirs = lax.ppermute(grown, axis, [(d, d ^ reach) for d in range(ways)])  89.7 us
    psum x4, blocking collectives, row_totals(): return lax.psum((sum_one, sum_two), 'col')  43.2 us
    reduce_scatter x1, waiting for transfers between devices, body(): lax.psum_scatter(grad_terms[2].astype(jnp.bfloat16), 'row', scatter_dimen...  33.7 us
    reduce_scatter x1, waiting for transfers between devices, body(): lax.psum_scatter(grad_terms[0].astype(jnp.bfloat16), 'row', scatter_dimen...  30.5 us
    psum x1, blocking collectives, body(): lax.psum((jnp.stack([jnp.sum(grad_qkv_f[:, 0], axis=0), jnp.sum(grad_qkv_...  24.8 us
    psum x1, waiting for transfers between devices, body(): lax.psum(shares[0].astype(jnp.bfloat16), 'img').astype(jnp.float32)  15 us
    reduce_scatter x1, waiting for transfers between devices, body(): lax.psum_scatter(grad_terms[3].astype(jnp.bfloat16), 'row', scatter_dimen...  12.3 us
  transfers between devices with their start and end apart: 20, of which 16 were waited for; matrix products, arithmetic and copies ran while one was open for 14% of the time, Pallas kernels for 0%

profile of v1, /device:TPU:0, one launch (start us, length us, event | category | flops | bytes accessed | tf_op | source)
XLA Modules:
  0.0 483.4 jit_solution(8107249804830968896)
XLA Ops:
  8.0 1.2 convert_reduce_fusion.1
  9.2 13.8 %all-reduce.4 = (f32[514,1]{0,1:T(1,128)S(1)}, f32[514,1]{0,1:T(1,128)S(1)}) all-reduce(f32[514,1]{0,1:T(1,128)S(1)} %broadcast_in_dim.16, f32[514,1]{0,1:T(1,128)S(1)} %broadcast_in_dim.17), channel_id=1, replica_groups=mesh['img'=2,'row'=4,'col'=4] {'col'}, use_global_device_ids=true, to_apply=%region_1.0 | all-reduce | flops 1028 | bytes 8224 | tf_op jit(solution)/shard_map/psum | solution.py:37
  23.1 1.2 fusion.38
  24.4 6.4 %collective-permute-done = bf16[514,256]{1,0:T(8,128)(2,1)S(1)} collective-permute-done((bf16[514,256]{1,0:T(8,128)(2,1)S(1)}, bf16[514,256]{1,0:T(8,128)(2,1)S(1)}, u32[]{:S(2)}, u32[]{:S(2)}) %collective-permute-start) | collective-permute-done | bytes 263200 | tf_op jit(solution)/shard_map/ppermute | solution.py:18
  31.0 2.2 copy.51
  33.2 7.6 %all_gather.17 = bf16[1024,256]{1,0:T(8,128)(2,1)} all-gather(bf16[256,256]{1,0:T(8,128)(2,1)S(1)} %copy-done.19), channel_id=1, replica_groups=mesh['img'=2,'row'=4,'col'=4] {'row'}, dimensions={0}, use_global_device_ids=true | all-gather | bytes 655360 | tf_op jit(solution)/shard_map/all_gather | solution.py:167
  40.9 13.1 %collective-permute-done.1 = bf16[514,512]{1,0:T(8,128)(2,1)S(1)} collective-permute-done((bf16[514,512]{1,0:T(8,128)(2,1)S(1)}, bf16[514,512]{1,0:T(8,128)(2,1)S(1)}, u32[]{:S(2)}, u32[]{:S(2)}) %collective-permute-start.1) | collective-permute-done | bytes 526368 | tf_op jit(solution)/shard_map/ppermute | solution.py:18
  53.9 2.6 fusion.22
  57.0 1.1 copy.49
  58.3 1.1 copy.50
  59.7 1.1 copy.52
  60.8 2.6 fusion
  64.8 1.2 copy-done.3
  66.5 1.2 copy.54
  67.7 2.0 convert_element_type.114
  69.7 2.7 convolution_convert_fusion.5
  73.8 24.7 %reduce-scatter.9.cloned.1.call-done = bf16[514,256]{1,0:T(8,128)(2,1)} async-done(((bf16[514,1024]{1,0:T(8,128)(2,1)}), bf16[514,256]{1,0:T(8,128)(2,1)}) %reduce-scatter.9.cloned.1.call-update) | async-done | bytes 263184 | tf_op jit(solution)/shard_map/reduce_scatter | solution.py:31
  98.5 1.2 fusion.51
  99.8 10.2 %all-reduce.3 = (f32[514,1]{0,1:T(1,128)}, f32[514,1]{0,1:T(1,128)}) all-reduce(f32[514,1]{0,1:T(1,128)S(1)} %broadcast_in_dim.18, f32[514,1]{0,1:T(1,128)S(1)} %broadcast_in_dim.19), channel_id=1, replica_groups=mesh['img'=2,'row'=4,'col'=4] {'col'}, use_global_device_ids=true, to_apply=%region_8.9 | all-reduce | flops 1028 | bytes 8224 | tf_op jit(solution)/shard_map/psum | solution.py:37
  110.8 1.2 add_convert_fusion
  113.0 5.4 %collective-permute-done.2 = bf16[514,256]{1,0:T(8,128)(2,1)S(1)} collective-permute-done((bf16[514,256]{1,0:T(8,128)(2,1)S(1)}, bf16[514,256]{1,0:T(8,128)(2,1)S(1)}, u32[]{:S(2)}, u32[]{:S(2)}) %collective-permute-start.2) | collective-permute-done | bytes 263200 | tf_op jit(solution)/shard_map/ppermute | solution.py:18
  120.1 1.7 collective-permute-start.4
  121.8 12.3 %collective-permute-done.4 = bf16[514,256]{1,0:T(8,128)(2,1)S(1)} collective-permute-done((bf16[514,256]{1,0:T(8,128)(2,1)S(1)}, bf16[514,256]{1,0:T(8,128)(2,1)S(1)}, u32[]{:S(2)}, u32[]{:S(2)}) %collective-permute-start.4) | collective-permute-done | bytes 263200 | tf_op jit(solution)/shard_map/ppermute | solution.py:18
  135.1 3.9 collective-permute-start.5
  139.0 15.6 %collective-permute-done.3 = bf16[514,512]{1,0:T(8,128)(2,1)} collective-permute-done((bf16[514,512]{1,0:T(8,128)(2,1)}, bf16[514,512]{1,0:T(8,128)(2,1)}, u32[]{:S(2)}, u32[]{:S(2)}) %collective-permute-start.3) | collective-permute-done | bytes 526368 | tf_op jit(solution)/shard_map/ppermute | solution.py:18
  154.6 5.4 %multiply_convert_fusion.1 = (bf16[514,1024]{1,0:T(8,128)(2,1)}, f32[514,1024]{1,0:T(8,128)}) fusion(f32[1024]{0:T(1024)} %param.29, bf16[1024,1024]{1,0:T(8,128)(2,1)} %all-gather.6.cloned.1.call-done, bf16[514,512]{1,0:T(8,128)(2,1)} %collective-permute-done.3, bf16[514,512]{1,0:T(8,128)(2,1)} %maximum_select_fusion.5, pred[]{:T(512)S(6)} %eq.4), kind=kOutput, calls=%fused_computation.15 | convolution fusion | flops 1085831168 | bytes 6311937 | tf_op jit(solution)/shard_map/dot_general | solution.py:183
  160.0 5.5 %collective-permute-done.5 = bf16[514,512]{1,0:T(8,128)(2,1)} collective-permute-done((bf16[514,512]{1,0:T(8,128)(2,1)}, bf16[514,512]{1,0:T(8,128)(2,1)}, u32[]{:S(2)}, u32[]{:S(2)}) %collective-permute-start.5) | collective-permute-done | bytes 526368 | tf_op jit(solution)/shard_map/ppermute | solution.py:18
  165.6 5.5 %convert_reduce_fusion = (f32[1024]{0:T(1024)}, bf16[514,1024]{1,0:T(8,128)(2,1)S(1)}) fusion(f32[514,1024]{1,0:T(8,128)} %get-tuple-element.71, f32[1024]{0:T(1024)S(1)} %copy-done.35, bf16[1024,1024]{1,0:T(8,128)(2,1)} %all-gather.8.cloned.1.call-done, bf16[514,512]{1,0:T(8,128)(2,1)} %collective-permute-done.5, ...), kind=kOutput, calls=%fused_computation.14 | convolution fusion | flops 1089514496 | bytes 6316033 | tf_op jit(solution)/shard_map/dot_general | solution.py:194
  172.1 2.3 convolution_convert_fusion.3
  174.4 4.2 convolution_convert_fusion.4
  178.8 22.2 %reduce-scatter.13.cloned.1.call-done = bf16[514,256]{1,0:T(8,128)(2,1)} async-done(((bf16[514,1024]{1,0:T(8,128)(2,1)}), bf16[514,256]{1,0:T(8,128)(2,1)}) %reduce-scatter.13.cloned.1.call-update) | async-done | bytes 263184 | tf_op jit(solution)/shard_map/reduce_scatter | solution.py:31
  200.9 2.1 fusion.32
  203.0 10.0 %all-reduce.2 = (f32[514,1]{0,1:T(1,128)}, f32[514,1]{0,1:T(1,128)}) all-reduce(f32[514,1]{0,1:T(1,128)S(1)} %broadcast_in_dim.21, f32[514,1]{0,1:T(1,128)S(1)} %broadcast_in_dim.20), channel_id=1, replica_groups=mesh['img'=2,'row'=4,'col'=4] {'col'}, use_global_device_ids=true, to_apply=%region_16.17 | all-reduce | flops 1028 | bytes 8224 | tf_op jit(solution)/shard_map/psum | solution.py:37
  213.7 15.7 %reduce-scatter.11.cloned.1.call-done = bf16[514,256]{1,0:T(8,128)(2,1)} async-done(((bf16[514,1024]{1,0:T(8,128)(2,1)}), bf16[514,256]{1,0:T(8,128)(2,1)}) %reduce-scatter.11.cloned.1.call-update) | async-done | bytes 263184 | tf_op jit(solution)/shard_map/reduce_scatter | solution.py:31
  229.4 3.2 multiply_reduce_fusion.2
  233.5 7.7 %collective-permute-done.6 = bf16[514,256]{1,0:T(8,128)(2,1)S(1)} collective-permute-done((bf16[514,256]{1,0:T(8,128)(2,1)S(1)}, bf16[514,256]{1,0:T(8,128)(2,1)S(1)}, u32[]{:S(2)}, u32[]{:S(2)}) %collective-permute-start.6) | collective-permute-done | bytes 263200 | tf_op jit(solution)/shard_map/ppermute | solution.py:18
  241.4 1.3 collective-permute-start.7
  242.8 23.6 %collective-permute-done.7 = bf16[514,512]{1,0:T(8,128)(2,1)S(1)} collective-permute-done((bf16[514,512]{1,0:T(8,128)(2,1)S(1)}, bf16[514,512]{1,0:T(8,128)(2,1)S(1)}, u32[]{:S(2)}, u32[]{:S(2)}) %collective-permute-start.7) | collective-permute-done | bytes 526368 | tf_op jit(solution)/shard_map/ppermute | solution.py:18
  267.2 1.5 convolution_convert_fusion.6
  268.8 5.1 %convolution_convert_fusion = bf16[1024,1024]{1,0:T(8,128)(2,1)} fusion(bf16[514,1024]{1,0:T(8,128)(2,1)} %get-tuple-element.70, bf16[514,512]{1,0:T(8,128)(2,1)} %collective-permute-done.5, bf16[514,512]{1,0:T(8,128)(2,1)} %maximum_select_fusion.6, pred[]{:T(512)S(6)} %eq.4), kind=kOutput, calls=%fused_computation.17 | convolution fusion | flops 1083721728 | bytes 4202497 | tf_op jit(solution)/shard_map/dot_general | solution.py:66
  273.9 5.1 %convolution_convert_fusion.1 = bf16[1024,1024]{1,0:T(8,128)(2,1)} fusion(bf16[514,1024]{1,0:T(8,128)(2,1)} %copy-done.36, bf16[514,512]{1,0:T(8,128)(2,1)} %collective-permute-done.3, bf16[514,512]{1,0:T(8,128)(2,1)} %maximum_select_fusion.5, pred[]{:T(512)S(6)} %eq.4), kind=kOutput, calls=%fused_computation.18 | convolution fusion | flops 1083721728 | bytes 4202497 | tf_op jit(solution)/shard_map/dot_general | solution.py:66
  279.3 2.8 convolution_convert_fusion.9
  282.2 2.1 reshape.89
  284.2 2.1 copy.56
  286.3 3.0 fusion.11
  289.4 2.1 copy.76
  291.5 2.1 reshape.85
  293.6 2.9 multiply_reduce_fusion
  297.5 1.2 copy-done.4
  302.9 3.9 convolution_convert_fusion.2
  306.9 3.5 bitcast_convert_fusion
  310.5 12.3 %reduce-scatter.23.cloned.1.call-done = bf16[256,1024]{1,0:T(8,128)(2,1)} async-done(((bf16[1024,1024]{1,0:T(8,128)(2,1)}), bf16[256,1024]{1,0:T(8,128)(2,1)}) %reduce-scatter.23.cloned.1.call-update) | async-done | bytes 524304 | tf_op jit(solution)/shard_map/reduce_scatter | solution.py:223
  322.8 33.7 %reduce-scatter.21.cloned.1.call-done = bf16[256,1024]{1,0:T(8,128)(2,1)} async-done(((bf16[1024,1024]{1,0:T(8,128)(2,1)}), bf16[256,1024]{1,0:T(8,128)(2,1)}) %reduce-scatter.21.cloned.1.call-update) | async-done | bytes 524304 | tf_op jit(solution)/shard_map/reduce_scatter | solution.py:220
  356.5 30.5 %reduce-scatter.17.cloned.1.call-done = bf16[256,3,256]{2,0,1:T(8,128)(2,1)} async-done(((bf16[1024,3,256]{2,0,1:T(8,128)(2,1)}), bf16[256,3,256]{2,0,1:T(8,128)(2,1)}) %reduce-scatter.17.cloned.1.call-update) | async-done | bytes 393232 | tf_op jit(solution)/shard_map/reduce_scatter | solution.py:214
  387.4 29.7 %reduce-scatter.15.cloned.1.call-done = bf16[514,256]{1,0:T(8,128)(2,1)} async-done(((bf16[514,1024]{1,0:T(8,128)(2,1)}), bf16[514,256]{1,0:T(8,128)(2,1)}) %reduce-scatter.15.cloned.1.call-update) | async-done | bytes 263184 | tf_op jit(solution)/shard_map/reduce_scatter | solution.py:31
  417.1 1.4 fusion.33
  418.6 24.8 %all-reduce = (f32[2,256]{1,0:T(2,128)}, f32[256]{0:T(256)}, f32[256]{0:T(256)}, f32[1024]{0:T(1024)}, f32[256]{0:T(256)}, /*index=5*/f32[256]{0:T(256)}, f32[25...) all-reduce(f32[2,256]{1,0:T(2,128)S(1)} %pad_maximum_fusion, ...), channel_id=1, replica_groups=mesh['img'=2,'row'=4,'col'=4] {'img','row'}, use_global_device_ids=true, to_apply=%region_27.28 | all-reduce | flops 3584 | bytes 28672 | tf_op jit(solution)/shard_map/psum | solution.py:234
  443.3 9.2 %all-reduce.1 = (f32[514,1]{0,1:T(1,128)S(1)}, f32[514,1]{0,1:T(1,128)S(1)}) all-reduce(f32[514,1]{0,1:T(1,128)S(1)} %broadcast_in_dim.23, f32[514,1]{0,1:T(1,128)S(1)} %broadcast_in_dim.22), channel_id=1, replica_groups=mesh['img'=2,'row'=4,'col'=4] {'col'}, use_global_device_ids=true, to_apply=%region_22.23 | all-reduce | flops 1028 | bytes 8224 | tf_op jit(solution)/shard_map/psum | solution.py:37
  452.5 2.1 fusion.26
  454.6 15.0 %all-reduce.8.cloned.1.call-done = (bf16[256,3,256]{2,0,1:T(8,128)(2,1)}, bf16[256,256]{1,0:T(8,128)(2,1)}, bf16[256,1024]{1,0:T(8,128)(2,1)}, bf16[256,1024]{1,0:T(8,128)(2,1)}) async-done(((bf16[256,3,256]{2,0,1:T(8,128)(2,1)}, bf16[256,256]{1,0:T(8,128)(2,1)}, bf16[256,1024]{1,0:T(8,128)(2,1)}, bf16[256,1024]{1,0:T(8,128)(2,1)}), (bf16[256,3,256]{2,0,1:T(8,128)(2,1)}, bf16[256,256]{1,0:T(8,128)(2,1)}, ...) | async-done | bytes 1572880 | tf_op jit(solution)/shard_map/psum | solution.py:228
  469.7 1.7 convert_element_type.134
  471.4 1.9 convert_element_type.131
  473.3 2.1 convert_element_type.136
  475.4 1.1 convert_element_type.139
  (147 shorter events, 19.2 us)
Async XLA Ops:
  7.2 23.8 %copy-start.14 = (bf16[4,257,257]{2,0,1:T(4,128)(2,1)S(1)}, bf16[4,257,257]{2,0,1:T(4,128)(2,1)}, u32[]{:S(2)}) copy-start(bf16[4,257,257]{2,0,1:T(4,128)(2,1)} %param.18) | copy-start | bytes 1585180
  7.2 46.7 %all-gather.4.cloned.1.call-start = ((), (), s32[]{:S(2)}) async-start(), calls=%async_computation.8 | async-start | bytes 1966080 | tf_op jit(solution)/shard_map/all_gather | solution.py:166
  7.9 90.6 %reduce-scatter.9.cloned.1.call-start = ((), (), s32[]{:S(2)}) async-start(), calls=%async_computation.9 | async-start | bytes 1331200 | tf_op jit(solution)/shard_map/reduce_scatter | solution.py:31
  9.2 24.1 %copy-start.19 = (bf16[256,256]{1,0:T(8,128)(2,1)S(1)}, bf16[256,256]{1,0:T(8,128)(2,1)}, u32[]{:S(2)}) copy-start(bf16[256,256]{1,0:T(8,128)(2,1)} %param.23) | copy-start | bytes 393220
  24.3 16.6 %copy-start.31 = (f32[2,256]{1,0:T(2,128)S(1)}, f32[2,256]{1,0:T(2,128)}, u32[]{:S(2)}) copy-start(f32[2,256]{1,0:T(2,128)} %param.22) | copy-start | bytes 6148
  24.3 6.5 %collective-permute-start = (bf16[514,256]{1,0:T(8,128)(2,1)S(1)}, bf16[514,256]{1,0:T(8,128)(2,1)S(1)}, u32[]{:S(2)}, u32[]{:S(2)}) collective-permute-start(bf16[514,256]{1,0:T(8,128)(2,1)S(1)} %fusion.38), channel_id=1, source_target_pairs={{0,1},{1,0},{2,3},{3,2},{4,5},{5,4},{6,7},{7,6},{8,9},{9,8},{10,11... | collective-permute-start | bytes 789512 | tf_op jit(solution)/shard_map/ppermute | solution.py:18
  30.9 23.0 %copy-start.15 = (bf16[514,512]{1,0:T(8,128)(2,1)}, bf16[514,512]{1,0:T(8,128)(2,1)S(1)}, u32[]{:S(2)}) copy-start(bf16[514,512]{1,0:T(8,128)(2,1)S(1)} %maximum_select_fusion.4) | copy-start | bytes 1579012
  30.9 23.0 %collective-permute-start.1 = (bf16[514,512]{1,0:T(8,128)(2,1)S(1)}, bf16[514,512]{1,0:T(8,128)(2,1)S(1)}, u32[]{:S(2)}, u32[]{:S(2)}) collective-permute-start(bf16[514,512]{1,0:T(8,128)(2,1)S(1)} %maximum_select_fusion.4), channel_id=1, source_target_pairs={{0,2},{1,3},{2,0},{3,1},{4,6},{5,7},{6,4},{7,5},{8,10},{9,11},{10,... | collective-permute-start | bytes 1579016 | tf_op jit(solution)/shard_map/ppermute | solution.py:18
  53.9 2.6 copy-start.33
  60.8 2.6 copy-start
  64.1 1.9 copy-start.8
  64.8 1.2 copy-start.3
  69.7 28.9 %copy-start.2 = (bf16[514,256]{1,0:T(8,128)(2,1)S(1)}, bf16[514,256]{1,0:T(8,128)(2,1)}, u32[]{:S(2)}) copy-start(bf16[514,256]{1,0:T(8,128)(2,1)} %param.17) | copy-start | bytes 789508
  69.7 28.9 %copy-start.20 = (f32[256]{0:T(256)S(1)}, f32[256]{0:T(256)}, u32[]{:S(2)}) copy-start(f32[256]{0:T(256)} %param.25) | copy-start | bytes 3076
  69.7 28.9 %copy-start.21 = (f32[256]{0:T(256)S(1)}, f32[256]{0:T(256)}, u32[]{:S(2)}) copy-start(f32[256]{0:T(256)} %param.24) | copy-start | bytes 3076
  69.7 41.1 %copy-start.22 = (f32[256]{0:T(256)S(1)}, f32[256]{0:T(256)}, u32[]{:S(2)}) copy-start(f32[256]{0:T(256)} %param.26) | copy-start | bytes 3076
  72.4 66.6 %all-gather.6.cloned.1.call-start = ((), (), s32[]{:S(2)}) async-start(), calls=%async_computation.10 | async-start | bytes 2621440 | tf_op jit(solution)/shard_map/all_gather | solution.py:168
  73.2 92.4 %all-gather.8.cloned.1.call-start = ((), (), s32[]{:S(2)}) async-start(), calls=%async_computation.11 | async-start | bytes 2621440 | tf_op jit(solution)/shard_map/all_gather | solution.py:169
  73.8 127.2 %reduce-scatter.13.cloned.1.call-start = ((), (), s32[]{:S(2)}) async-start(), calls=%async_computation.13 | async-start | bytes 1331200 | tf_op jit(solution)/shard_map/reduce_scatter | solution.py:31
  110.0 9.4 %copy-start.11 = (f32[514,256]{1,0:T(8,128)S(1)}, f32[514,256]{1,0:T(8,128)}, u32[]{:S(2)}) copy-start(f32[514,256]{1,0:T(8,128)} %param.33) | copy-start | bytes 1579012
  112.0 6.5 %collective-permute-start.2 = (bf16[514,256]{1,0:T(8,128)(2,1)S(1)}, bf16[514,256]{1,0:T(8,128)(2,1)S(1)}, u32[]{:S(2)}, u32[]{:S(2)}) collective-permute-start(bf16[514,256]{1,0:T(8,128)(2,1)S(1)} %add_convert_fusion), channel_id=1, source_target_pairs={{0,1},{1,0},{2,3},{3,2},{4,5},{5,4},{6,7},{7,6},{8,9},{9,8},{10,11... | collective-permute-start | bytes 789512 | tf_op jit(solution)/shard_map/ppermute | solution.py:18
  119.4 35.2 %collective-permute-start.3 = (bf16[514,512]{1,0:T(8,128)(2,1)}, bf16[514,512]{1,0:T(8,128)(2,1)}, u32[]{:S(2)}, u32[]{:S(2)}) collective-permute-start(bf16[514,512]{1,0:T(8,128)(2,1)} %maximum_select_fusion.5), channel_id=1, source_target_pairs={{0,2},{1,3},{2,0},{3,1},{4,6},{5,7},{6,4},{7,5},{8,10},{9,11},{10,... | collective-permute-start | bytes 1579016 | tf_op jit(solution)/shard_map/ppermute | solution.py:18
  120.1 14.0 %collective-permute-start.4 = (bf16[514,256]{1,0:T(8,128)(2,1)S(1)}, bf16[514,256]{1,0:T(8,128)(2,1)S(1)}, u32[]{:S(2)}, u32[]{:S(2)}) collective-permute-start(bf16[514,256]{1,0:T(8,128)(2,1)S(1)} %multiply_convert_fusion.3), channel_id=1, source_target_pairs={{0,1},{1,0},{2,3},{3,2},{4,5},{5,4},{6,7},{7,6},{8,9},{9,8},{10,11... | collective-permute-start | bytes 789512 | tf_op jit(solution)/shard_map/ppermute | solution.py:18
  135.1 30.5 %copy-start.35 = (f32[1024]{0:T(1024)S(1)}, f32[1024]{0:T(1024)}, u32[]{:S(2)}) copy-start(f32[1024]{0:T(1024)} %param.29) | copy-start | bytes 12292
  135.1 30.5 %collective-permute-start.5 = (bf16[514,512]{1,0:T(8,128)(2,1)}, bf16[514,512]{1,0:T(8,128)(2,1)}, u32[]{:S(2)}, u32[]{:S(2)}) collective-permute-start(bf16[514,512]{1,0:T(8,128)(2,1)} %maximum_select_fusion.6), channel_id=1, source_target_pairs={{0,2},{1,3},{2,0},{3,1},{4,6},{5,7},{6,4},{7,5},{8,10},{9,11},{10,... | collective-permute-start | bytes 1579016 | tf_op jit(solution)/shard_map/ppermute | solution.py:18
  165.6 6.5 %copy-start.32 = (bf16[1024,1024]{1,0:T(8,128)(2,1)S(1)}, bf16[1024,1024]{1,0:T(8,128)(2,1)}, u32[]{:S(2)}) copy-start(bf16[1024,1024]{1,0:T(8,128)(2,1)} %all-gather.6.cloned.1.call-done) | copy-start | bytes 6291460
  171.1 1.0 copy-start.36
  174.4 55.0 %reduce-scatter.11.cloned.1.call-start = ((), (), s32[]{:S(2)}) async-start(), calls=%async_computation.12 | async-start | bytes 1331200 | tf_op jit(solution)/shard_map/reduce_scatter | solution.py:31
  178.7 131.8 %reduce-scatter.19.cloned.1.call-start = ((), (), s32[]{:S(2)}) async-start(), calls=%async_computation.16 | async-start | bytes 655360 | tf_op jit(solution)/shard_map/reduce_scatter | solution.py:217
  229.4 37.7 %copy-start.12 = (bf16[514,256]{0,1:T(8,128)(2,1)S(1)}, bf16[514,256]{0,1:T(8,128)(2,1)}, u32[]{:S(2)}) copy-start(bf16[514,256]{0,1:T(8,128)(2,1)} %convert_element_type.114) | copy-start | bytes 789508
  232.6 0.8 copy-start.6
  233.4 7.8 %collective-permute-start.6 = (bf16[514,256]{1,0:T(8,128)(2,1)S(1)}, bf16[514,256]{1,0:T(8,128)(2,1)S(1)}, u32[]{:S(2)}, u32[]{:S(2)}) collective-permute-start(bf16[514,256]{1,0:T(8,128)(2,1)S(1)} %multiply_convert_fusion.2), channel_id=1, source_target_pairs={{0,1},{1,0},{2,3},{3,2},{4,5},{5,4},{6,7},{7,6},{8,9},{9,8},{10,11... | collective-permute-start | bytes 789512 | tf_op jit(solution)/shard_map/ppermute | solution.py:18
  241.4 25.0 %copy-start.17 = (bf16[514,512]{1,0:T(8,128)(2,1)}, bf16[514,512]{1,0:T(8,128)(2,1)S(1)}, u32[]{:S(2)}) copy-start(bf16[514,512]{1,0:T(8,128)(2,1)S(1)} %maximum_select_fusion.7) | copy-start | bytes 1579012
  241.4 25.0 %collective-permute-start.7 = (bf16[514,512]{1,0:T(8,128)(2,1)S(1)}, bf16[514,512]{1,0:T(8,128)(2,1)S(1)}, u32[]{:S(2)}, u32[]{:S(2)}) collective-permute-start(bf16[514,512]{1,0:T(8,128)(2,1)S(1)} %maximum_select_fusion.7), channel_id=1, source_target_pairs={{0,2},{1,3},{2,0},{3,1},{4,6},{5,7},{6,4},{7,5},{8,10},{9,11},{10,... | collective-permute-start | bytes 1579016 | tf_op jit(solution)/shard_map/ppermute | solution.py:18
  266.4 0.8 copy-start.34
  268.7 54.1 %reduce-scatter.23.cloned.1.call-start = ((), (), s32[]{:S(2)}) async-start(), calls=%async_computation.18 | async-start | bytes 2621440 | tf_op jit(solution)/shard_map/reduce_scatter | solution.py:223
  273.9 82.6 %reduce-scatter.21.cloned.1.call-start = ((), (), s32[]{:S(2)}) async-start(), calls=%async_computation.17 | async-start | bytes 2621440 | tf_op jit(solution)/shard_map/reduce_scatter | solution.py:220
  279.1 108.0 %reduce-scatter.17.cloned.1.call-start = ((), (), s32[]{:S(2)}) async-start(), calls=%async_computation.15 | async-start | bytes 1966080 | tf_op jit(solution)/shard_map/reduce_scatter | solution.py:214
  293.6 3.0 copy-start.1
  296.6 2.2 copy-start.10
  297.5 1.2 copy-start.4
  298.7 1.3 copy-start.9
  299.2 1.5 copy-start.5
  300.8 1.6 copy-start.13
  301.9 1.0 copy-start.16
  306.9 110.2 %reduce-scatter.15.cloned.1.call-start = ((), (), s32[]{:S(2)}) async-start(), calls=%async_computation.14 | async-start | bytes 1331200 | tf_op jit(solution)/shard_map/reduce_scatter | solution.py:31
  310.4 159.3 %all-reduce.8.cloned.1.call-start = ((), (), s32[]{:S(2)}) async-start(), calls=%async_computation.19 | async-start | bytes 3145728 | tf_op jit(solution)/shard_map/psum | solution.py:228
  387.0 30.0 %copy-start.23 = (f32[256]{0:T(256)S(1)}, f32[256]{0:T(256)}, u32[]{:S(2)}) copy-start(f32[256]{0:T(256)} %param.19) | copy-start | bytes 3076
  387.0 31.4 %copy-start.24 = (f32[256]{0:T(256)S(1)}, f32[256]{0:T(256)}, u32[]{:S(2)}) copy-start(f32[256]{0:T(256)} %get-tuple-element.26) | copy-start | bytes 3076
  387.1 31.4 %copy-start.25 = (f32[256]{0:T(256)S(1)}, f32[256]{0:T(256)}, u32[]{:S(2)}) copy-start(f32[256]{0:T(256)} %get-tuple-element.27) | copy-start | bytes 3076
  387.1 31.4 %copy-start.26 = (f32[256]{0:T(256)S(1)}, f32[256]{0:T(256)}, u32[]{:S(2)}) copy-start(f32[256]{0:T(256)} %get-tuple-element.64) | copy-start | bytes 3076
  387.1 31.4 %copy-start.27 = (f32[256]{0:T(256)S(1)}, f32[256]{0:T(256)}, u32[]{:S(2)}) copy-start(f32[256]{0:T(256)} %get-tuple-element.65) | copy-start | bytes 3076
  387.1 31.4 %copy-start.28 = (f32[256]{0:T(256)S(1)}, f32[256]{0:T(256)}, u32[]{:S(2)}) copy-start(f32[256]{0:T(256)} %get-tuple-element.18) | copy-start | bytes 3076
  387.1 31.4 %copy-start.29 = (f32[256]{0:T(256)S(1)}, f32[256]{0:T(256)}, u32[]{:S(2)}) copy-start(f32[256]{0:T(256)} %get-tuple-element.30) | copy-start | bytes 3076
  387.1 31.4 %copy-start.30 = (f32[1024]{0:T(1024)S(1)}, f32[1024]{0:T(1024)}, u32[]{:S(2)}) copy-start(f32[1024]{0:T(1024)} %get-tuple-element.74) | copy-start | bytes 12292
  387.1 65.4 %copy-start.7 = (f32[514,256]{1,0:T(8,128)S(1)}, f32[514,256]{1,0:T(8,128)}, u32[]{:S(2)}) copy-start(f32[514,256]{1,0:T(8,128)} %copy-done.6) | copy-start | bytes 1579012
  469.7 5.8 %copy-start.18 = (bf16[256,1024]{1,0:T(8,128)(2,1)S(1)}, bf16[256,1024]{1,0:T(8,128)(2,1)}, u32[]{:S(2)}) copy-start(bf16[256,1024]{1,0:T(8,128)(2,1)} %get-tuple-element.59) | copy-start | bytes 1572868
Sparse Core Ops, SparseCore 0:
  9.6 22.3 all-gather.3
  72.6 25.9 reduce-scatter.8
  100.1 21.0 all-gather.5
  122.6 22.5 all-gather.7
  174.5 26.3 reduce-scatter.12
  203.1 26.3 reduce-scatter.10
  268.8 20.2 reduce-scatter.18
  291.6 31.1 reduce-scatter.22
  325.3 31.1 reduce-scatter.20
  358.9 28.0 reduce-scatter.16
  389.3 27.6 reduce-scatter.14
  419.4 50.2 all-reduce.7
